TPU v7x, 32 devices: a whole 2x2x4 slice. The times are simulated.
32 devices in a mesh: dp: 8 (over z, x), mp: 4 (over y, core).
Axes of the slice: x: 2, y: 2, z: 4, core: 2. Of those that a mesh axis runs over, the one named last changes fastest.
Arguments:
- patches: bfloat16 [32000, 768], P(('dp', 'mp')), may hold values from -6 to 6
- dataset_id: int32 [160], P('dp'), may hold values from 0 to 7
- patch_masks: int32 [8, 200], replicated, may hold values 0 or 1
- mask_tokens: bfloat16 [8, 768], replicated, may hold values from -6 to 6
- key_mask: int32 [160, 200], P('dp'), may hold values from 0 to 1, as said below
- bias_index: int32 [200, 200], replicated, may hold values from 0 to 731
- norm1_gain: float32 [768], replicated, may hold values from 0.5 to 1.5
- norm1_shift: float32 [768], replicated, may hold values from -1.8 to 1.8
- qkv_weight: bfloat16 [768, 3, 768], P(None, None, 'mp'), may hold values from -0.21875 to 0.21875
- query_bias: bfloat16 [768], P('mp'), may hold values from -3 to 3
- value_bias: bfloat16 [768], P('mp'), may hold values from -3 to 3
- bias_table: bfloat16 [732, 12], P(None, 'mp'), may hold values from -5 to 5
- out_weight: bfloat16 [768, 768], P('mp'), may hold values from -1.75 to 1.75
- out_bias: float32 [768], replicated, may hold values from -1.8 to 1.8
- gamma_attn: float32 [768], replicated, may hold values from 0.5 to 2
- norm2_gain: float32 [768], replicated, may hold values from 0.5 to 1.5
- norm2_shift: float32 [768], replicated, may hold values from -1.8 to 1.8
- up_weight: bfloat16 [768, 3072], P(None, 'mp'), may hold values from -0.21875 to 0.21875
- up_bias: bfloat16 [3072], P('mp'), may hold values from -3 to 3
- down_weight: bfloat16 [3072, 768], P('mp'), may hold values from -0.109375 to 0.109375
- down_bias: float32 [768], replicated, may hold values from -1.8 to 1.8
- gamma_mlp: float32 [768], replicated, may hold values from 0.5 to 2
- cotangent: bfloat16 [32000, 768], P(('dp', 'mp')), may hold values from -6 to 6
Outputs:
- output: bfloat16 [32000, 768], P(('dp', 'mp'))
- patch_grad: float32 [32000, 768], P(('dp', 'mp'))
- token_grad: float32 [8, 768], replicated
- norm1_gain_grad: float32 [768], replicated
- norm1_shift_grad: float32 [768], replicated
- qkv_grad: float32 [768, 3, 768], P(None, None, 'mp')
- query_bias_grad: float32 [768], P('mp')
- value_bias_grad: float32 [768], P('mp')
- table_grad: float32 [732, 12], P(None, 'mp')
- out_weight_grad: float32 [768, 768], P('mp')
- out_bias_grad: float32 [768], replicated
- gamma_attn_grad: float32 [768], replicated
- norm2_gain_grad: float32 [768], replicated
- norm2_shift_grad: float32 [768], replicated
- up_weight_grad: float32 [768, 3072], P(None, 'mp')
- up_bias_grad: float32 [3072], P('mp')
- down_weight_grad: float32 [3072, 768], P('mp')
- down_bias_grad: float32 [768], replicated
- gamma_mlp_grad: float32 [768], replicated
Inputs may be any that keep to these rules, and one draw needn't show every extreme that they name: `key_mask`: each row holds ones on a prefix of its positions and zeros after it; the first position is always one.
All inputs are finite; a program needn't handle non-finite values.
Results may differ from a plain program's by a relative error of at most 0.013.
The roundings to bfloat16 on the way count: a program that leaves them out, or rounds other values in their place, can miss the bound.
Values may be sent and summed in bfloat16 or wider, within the bound.
No kernel may reach another device: no remote copies, remote signals or barrier semaphores. Data moves between devices by JAX's collectives and lax.ppermute only.
A program may use at most 192 MiB of HBM per device.

v0:
```python
import jax
import jax.numpy as jnp
from jax import lax
from jax.sharding import PartitionSpec as P

HEAD = 64
SEQ = 200
GROUPS = 8
IMG_BLK = 5


def layer_norm(values, gain, shift):
    mean = jnp.mean(values, axis=-1, keepdims=True)
    centred = values - mean
    spread = jnp.mean(centred * centred, axis=-1, keepdims=True)
    return centred * lax.rsqrt(spread + 1e-06) * gain + shift


def gelu_exact(values):
    return jax.nn.gelu(values, approximate=False)


def product(left, right):
    return jnp.dot(left, right, preferred_element_type=jnp.float32)


def product_first(left, right):
    return lax.dot_general(
        left, right, (((0,), (0,)), ((), ())), preferred_element_type=jnp.float32
    )


def product_last(left, right):
    return lax.dot_general(
        left, right, (((1,), (1,)), ((), ())), preferred_element_type=jnp.float32
    )


def product_cross(left, right):
    return lax.dot_general(
        left, right, (((0,), (1,)), ((), ())), preferred_element_type=jnp.float32
    )


def score_block(queries, keys, bias, key_mask):
    scores = (
        jnp.einsum("bqhe,bkhe->bhqk", queries, keys, preferred_element_type=jnp.float32)
        + bias[None]
    )
    return jnp.where(key_mask[:, None, None, :] > 0, scores, -1e30)


def attention_forward(normed, qkv_all, qbias_all, vbias_all, table_all, masks_here, position_table):
    width = qkv_all.shape[2]
    heads = width // HEAD
    images = masks_here.shape[0]
    scale = HEAD ** (-0.5)
    joint = product(normed, qkv_all.reshape(qkv_all.shape[0], 3 * width))
    shape5 = (images // IMG_BLK, IMG_BLK, SEQ, heads, HEAD)
    queries = (
        ((joint[:, :width] + qbias_all.astype(jnp.float32)) * scale)
        .astype(jnp.bfloat16)
        .reshape(shape5)
    )
    keys = joint[:, width : 2 * width].astype(jnp.bfloat16).reshape(shape5)
    values = (
        (joint[:, 2 * width :] + vbias_all.astype(jnp.float32)).astype(jnp.bfloat16).reshape(shape5)
    )
    bias_flat = product_cross(table_all, position_table)
    bias = bias_flat.reshape(heads, SEQ, SEQ)
    block_masks = masks_here.reshape(images // IMG_BLK, IMG_BLK, SEQ)

    def attend(pieces):
        block_q, block_k, block_v, block_mask = pieces
        scores = score_block(block_q, block_k, bias, block_mask)
        largest = jnp.max(scores, axis=-1, keepdims=True)
        lse = largest + jnp.log(jnp.sum(jnp.exp(scores - largest), axis=-1, keepdims=True))
        probs = jnp.exp(scores - lse).astype(jnp.bfloat16)
        context = jnp.einsum("bhqk,bkhe->bqhe", probs, block_v, preferred_element_type=jnp.float32)
        return (context.astype(jnp.bfloat16), lse)

    context, lse = lax.map(attend, (queries, keys, values, block_masks))
    return (queries, keys, values, block_masks, bias, context.reshape(images * SEQ, width), lse)


def attention_backward(queries, keys, values, block_masks, bias, lse, grad_context, position_table):
    heads = queries.shape[3]
    width = heads * HEAD
    scale = HEAD ** (-0.5)
    grad_blocks = grad_context.reshape(queries.shape)

    def step(total, pieces):
        block_q, block_k, block_v, block_mask, block_lse, block_grad = pieces
        scores = score_block(block_q, block_k, bias, block_mask)
        probs = jnp.exp(scores - block_lse)
        grad_probs = jnp.einsum(
            "bqhe,bkhe->bhqk", block_grad, block_v, preferred_element_type=jnp.float32
        )
        centre = jnp.sum(probs * grad_probs, axis=-1, keepdims=True)
        grad_scores = (probs * (grad_probs - centre)).astype(jnp.bfloat16)
        grad_values = jnp.einsum(
            "bhqk,bqhe->bkhe",
            probs.astype(jnp.bfloat16),
            block_grad,
            preferred_element_type=jnp.float32,
        ).astype(jnp.bfloat16)
        grad_queries = (
            jnp.einsum(
                "bhqk,bkhe->bqhe", grad_scores, block_k, preferred_element_type=jnp.float32
            ).astype(jnp.bfloat16)
            * scale
        )
        grad_keys = jnp.einsum(
            "bhqk,bqhe->bkhe", grad_scores, block_q, preferred_element_type=jnp.float32
        ).astype(jnp.bfloat16)
        total = total + jnp.sum(grad_scores.astype(jnp.float32), axis=0)
        return (total, (grad_queries, grad_keys, grad_values))

    start_total = jnp.zeros((heads, SEQ, SEQ), jnp.float32)
    total, (grad_q, grad_k, grad_v) = lax.scan(
        step, start_total, (queries, keys, values, block_masks, lse, grad_blocks)
    )
    rows = grad_context.shape[0]
    grad_q = grad_q.reshape(rows, width)
    grad_k = grad_k.reshape(rows, width)
    grad_v = grad_v.reshape(rows, width)
    grad_joint = jnp.concatenate([grad_q, grad_k, grad_v], axis=1)
    qbias_local = jnp.sum(grad_q.astype(jnp.float32), axis=0)
    vbias_local = jnp.sum(grad_v.astype(jnp.float32), axis=0)
    total_flat = total.reshape(heads, SEQ * SEQ)
    upper_part = total_flat.astype(jnp.bfloat16)
    lower_part = (total_flat - upper_part.astype(jnp.float32)).astype(jnp.bfloat16)
    stacked = jnp.concatenate([upper_part, lower_part], axis=0)
    table_both = product_cross(position_table, stacked)
    table_local = table_both[:, :heads] + table_both[:, heads:]
    return (grad_joint, qbias_local, vbias_local, table_local)


def local(
    patches,
    dataset_id,
    patch_masks,
    mask_tokens,
    key_mask,
    bias_index,
    norm1_gain,
    norm1_shift,
    qkv_weight,
    query_bias,
    value_bias,
    bias_table,
    out_weight,
    out_bias,
    gamma_attn,
    norm2_gain,
    norm2_shift,
    up_weight,
    up_bias,
    down_weight,
    down_bias,
    gamma_mlp,
    cotangent,
):
    rows = patches.shape[0]
    mp_count = lax.axis_size("mp")
    mp_place = lax.axis_index("mp")
    images = dataset_id.shape[0]
    own_images = images // mp_count
    table_rows = bias_table.shape[0]
    own_ids = lax.dynamic_slice_in_dim(dataset_id, mp_place * own_images, own_images, 0)
    own_choose = (own_ids[:, None] == jnp.arange(GROUPS)[None, :]).astype(jnp.bfloat16)
    own_sel = product(own_choose, patch_masks.astype(jnp.bfloat16))
    selected = own_sel.reshape(rows, 1)
    row_choose = jnp.broadcast_to(own_choose[:, None, :], (own_images, SEQ, GROUPS)).reshape(
        rows, GROUPS
    )
    token_rows = jnp.broadcast_to(
        product(own_choose, mask_tokens)[:, None, :], (own_images, SEQ, mask_tokens.shape[1])
    ).reshape(rows, mask_tokens.shape[1])
    position_table = (bias_index.reshape(SEQ * SEQ, 1) == jnp.arange(table_rows)[None, :]).astype(
        jnp.bfloat16
    )
    start = patches.astype(jnp.float32) * (1.0 - selected) + selected * token_rows
    norm1_value, norm1_back = jax.vjp(layer_norm, start, norm1_gain, norm1_shift)
    normed1 = norm1_value.astype(jnp.bfloat16)
    attn_in = lax.all_gather(normed1, "mp", axis=0, tiled=True)
    qkv_all, qbias_all, vbias_all, table_all, out_all = (
        qkv_weight,
        query_bias,
        value_bias,
        bias_table,
        out_weight,
    )
    queries, keys, values, block_masks, bias, context, lse = attention_forward(
        attn_in, qkv_all, qbias_all, vbias_all, table_all, key_mask, position_table
    )
    out_part = product(context, out_all)
    attn_sum = lax.psum_scatter(out_part, "mp", scatter_dimension=0, tiled=True)
    attn_value = attn_sum + out_bias
    middle = start + gamma_attn * attn_value
    norm2_value, norm2_back = jax.vjp(layer_norm, middle, norm2_gain, norm2_shift)
    normed2 = norm2_value.astype(jnp.bfloat16)
    mlp_in = lax.all_gather(normed2, "mp", axis=0, tiled=True)
    up_all, upb_all, down_all = (up_weight, up_bias, down_weight)
    hidden_pre = product(mlp_in, up_all) + upb_all.astype(jnp.float32)
    hidden_act, gelu_back = jax.vjp(gelu_exact, hidden_pre)
    hidden = hidden_act.astype(jnp.bfloat16)
    down_part = product(hidden, down_all)
    mlp_sum = lax.psum_scatter(
        down_part.astype(jnp.bfloat16), "mp", scatter_dimension=0, tiled=True
    ).astype(jnp.float32)
    mlp_value = mlp_sum + down_bias
    output = (middle + gamma_mlp * mlp_value).astype(jnp.bfloat16)
    grad_out = cotangent.astype(jnp.float32)
    gamma_mlp_part = jnp.sum(grad_out * mlp_value, axis=0)
    grad_mlp = (gamma_mlp * grad_out).astype(jnp.bfloat16)
    down_bias_part = jnp.sum(grad_mlp.astype(jnp.float32), axis=0)
    grad_mlp_all = lax.all_gather(grad_mlp, "mp", axis=0, tiled=True)
    down_grad_local = product_first(hidden, grad_mlp_all)
    grad_hidden = product_last(grad_mlp_all, down_all)
    grad_pre = gelu_back(grad_hidden)[0].astype(jnp.bfloat16)
    up_bias_local = jnp.sum(grad_pre.astype(jnp.float32), axis=0)
    up_grad_local = product_first(mlp_in, grad_pre)
    norm2_part = product_last(grad_pre, up_all)
    grad_normed2 = lax.psum_scatter(norm2_part, "mp", scatter_dimension=0, tiled=True)
    up_grad, up_bias_grad, down_grad = (up_grad_local, up_bias_local, down_grad_local)
    grad_middle_norm, norm2_gain_part, norm2_shift_part = norm2_back(grad_normed2)
    grad_middle = grad_out + grad_middle_norm
    gamma_attn_part = jnp.sum(grad_middle * attn_value, axis=0)
    grad_attn = (gamma_attn * grad_middle).astype(jnp.bfloat16)
    out_bias_part = jnp.sum(grad_attn.astype(jnp.float32), axis=0)
    grad_attn_all = lax.all_gather(grad_attn, "mp", axis=0, tiled=True)
    out_grad_local = product_first(context, grad_attn_all)
    grad_context = product_last(grad_attn_all, out_all).astype(jnp.bfloat16)
    grad_joint, qbias_local, vbias_local, table_local = attention_backward(
        queries, keys, values, block_masks, bias, lse, grad_context, position_table
    )
    width = qkv_all.shape[2]
    model_width = qkv_all.shape[0]
    qkv_grad_local = product_first(attn_in, grad_joint).reshape(model_width, 3, width)
    norm1_part = product_last(grad_joint, qkv_all.reshape(model_width, 3 * width))
    grad_normed1 = lax.psum_scatter(
        norm1_part.astype(jnp.bfloat16), "mp", scatter_dimension=0, tiled=True
    ).astype(jnp.float32)
    qkv_grad, qbias_grad, vbias_grad, table_grad, out_grad = (
        qkv_grad_local,
        qbias_local,
        vbias_local,
        table_local,
        out_grad_local,
    )
    grad_start_norm, norm1_gain_part, norm1_shift_part = norm1_back(grad_normed1)
    grad_start = grad_middle + grad_start_norm
    patch_grad = grad_start * (1.0 - selected)
    token_part = lax.dot_general(
        row_choose.astype(jnp.float32),
        grad_start * selected,
        (((0,), (0,)), ((), ())),
        precision=lax.Precision.HIGHEST,
    )
    qkv_grad, qbias_grad, vbias_grad, table_grad, out_grad, up_grad, up_bias_grad, down_grad = (
        lax.psum(
            (
                qkv_grad,
                qbias_grad,
                vbias_grad,
                table_grad,
                out_grad,
                up_grad,
                up_bias_grad,
                down_grad,
            ),
            "dp",
        )
    )
    (
        token_grad,
        norm1_gain_grad,
        norm1_shift_grad,
        out_bias_grad,
        gamma_attn_grad,
        norm2_gain_grad,
        norm2_shift_grad,
        down_bias_grad,
        gamma_mlp_grad,
    ) = lax.psum(
        (
            token_part,
            norm1_gain_part,
            norm1_shift_part,
            out_bias_part,
            gamma_attn_part,
            norm2_gain_part,
            norm2_shift_part,
            down_bias_part,
            gamma_mlp_part,
        ),
        ("dp", "mp"),
    )
    return (
        output,
        patch_grad,
        token_grad,
        norm1_gain_grad,
        norm1_shift_grad,
        qkv_grad,
        qbias_grad,
        vbias_grad,
        table_grad,
        out_grad,
        out_bias_grad,
        gamma_attn_grad,
        norm2_gain_grad,
        norm2_shift_grad,
        up_grad,
        up_bias_grad,
        down_grad,
        down_bias_grad,
        gamma_mlp_grad,
    )


def solution(mesh):
    return jax.shard_map(
        local,
        mesh=mesh,
        in_specs=(
            P(("dp", "mp"), None),
            P("dp"),
            P(),
            P(),
            P("dp", None),
            P(),
            P(),
            P(),
            P(None, None, "mp"),
            P("mp"),
            P("mp"),
            P(None, "mp"),
            P("mp", None),
            P(),
            P(),
            P(),
            P(),
            P(None, "mp"),
            P("mp"),
            P("mp", None),
            P(),
            P(),
            P(("dp", "mp"), None),
        ),
        out_specs=(
            P(("dp", "mp"), None),
            P(("dp", "mp"), None),
            P(),
            P(),
            P(),
            P(None, None, "mp"),
            P("mp"),
            P("mp"),
            P(None, "mp"),
            P("mp", None),
            P(),
            P(),
            P(),
            P(),
            P(None, "mp"),
            P("mp"),
            P("mp", None),
            P(),
            P(),
        ),
        check_vma=False,
    )
```

profile of v0, /device:TPU:0, one launch (start us, length us, event | category | flops | bytes accessed | tf_op | source)
XLA Modules:
  0.0 1081.7 jit_solution(13086309809975984235)
XLA Ops:
  22.6 18.9 %fusion.61 = f32[3,40000]{1,0:T(4,128)} fusion(bf16[732,3]{0,1:T(4,128)(2,1)S(1)} %copy-done.62, s32[40000]{0:T(1024)S(1)} %eq.35), kind=kOutput, calls=%fused_computation.71 | convolution fusion | flops 204960000 | bytes 644392 | tf_op jit(solution)/shard_map/dot_general | solution.py:40
  44.3 26.1 %all-gather.5.cloned.1.call-done = bf16[4000,768]{1,0:T(8,128)(2,1)} async-done(((bf16[1000,768]{1,0:T(8,128)(2,1)}), bf16[4000,768]{1,0:T(8,128)(2,1)}) %all-gather.5.cloned.1.call-update) | async-done | bytes 6144016 | tf_op jit(solution)/shard_map/all_gather | solution.py:186
  70.5 6.2 fusion.95
  80.6 7.3 reshape.237
  92.3 7.6 reshape.239
  104.5 7.3 reshape.240
  117.7 30.9 %while.31 = (s32[]{:T(128)}, bf16[4,5,200,3,64]{2,4,3,1,0:T(8,128)(2,1)}, f32[4,5,3,200,1]{3,2,1,4,0:T(4,128)}, bf16[4,5,200,3,64]{2,4,3,1,0:T(8,128)(2,1)}, s32...) while((s32[]{:T(128)}, ...), condition=%wide.wide.region_5.6_spmd, body=%wide.wide.region_2.5_spmd.sunk | while | flops 160390000 | bytes 11681225 | solution.py:82
  153.0 5.7 reshape.241
  158.8 7.7 fusion.96
  166.7 97.1 %reduce-scatter.5.cloned.1.call-done = f32[1000,768]{1,0:T(8,128)} async-done(((f32[4000,768]{1,0:T(8,128)}), f32[1000,768]{1,0:T(8,128)}) %reduce-scatter.5.cloned.1.call-update) | async-done | bytes 3072016 | tf_op jit(solution)/shard_map/reduce_scatter | solution.py:198
  277.0 43.4 %all-gather.7.cloned.1.call-done = bf16[4000,768]{1,0:T(8,128)(2,1)} async-done(((bf16[1000,768]{1,0:T(8,128)(2,1)}), bf16[4000,768]{1,0:T(8,128)(2,1)}) %all-gather.7.cloned.1.call-update) | async-done | bytes 6144016 | tf_op jit(solution)/shard_map/all_gather | solution.py:203
  320.4 13.8 %fusion.97 = f32[4000,768]{1,0:T(8,128)} fusion(bf16[4000,768]{1,0:T(8,128)(2,1)} %all-gather.7.cloned.1.call-done, bf16[768,768]{1,0:T(8,128)(2,1)} %param.44), kind=kOutput, calls=%fused_computation.165 | convolution fusion | flops 4718592000 | bytes 19611648 | tf_op jit(solution)/shard_map/dot_general | solution.py:24
  334.2 33.8 %all-gather.9.cloned.1.call-done = bf16[4000,768]{1,0:T(8,128)(2,1)} async-done(((bf16[1000,768]{1,0:T(8,128)(2,1)}), bf16[4000,768]{1,0:T(8,128)(2,1)}) %all-gather.9.cloned.1.call-update) | async-done | bytes 6144016 | tf_op jit(solution)/shard_map/all_gather | solution.py:218
  368.0 36.0 %convert_reduce_fusion.1 = (f32[768]{0:T(1024)}, bf16[4000,768]{1,0:T(8,128)(2,1)S(1)}, f32[4000,768]{1,0:T(8,128)}) fusion(f32[4000,768]{1,0:T(8,128)} %fusion.97, f32[768]{0:T(1024)S(1)} %convert_element_type.138, bf16[4000,768]{1,0:T(8,128)(2,1)} %all-gather.9.cloned.1.call-done, bf16[768,768]{1,0:T(8,128)(2,1)S(1)} %copy-done), kind=kOutput, calls=%fused_computation.74 | convolution fusion | flops 4948990976 | bytes 38049792 | tf_op jit(solution)/shard_map/dot_general | solution.py:34
  406.5 7.9 fusion.98
  414.7 11.1 %multiply_convert_fusion.1 = bf16[4000,768]{1,0:T(8,128)(2,1)S(1)} fusion(f32[4000,768]{1,0:T(8,128)} %get-tuple-element.343, f32[4000,768]{1,0:T(8,128)} %fusion.97, f32[768]{0:T(1024)S(1)} %convert_element_type.138), kind=kLoop, calls=%fused_computation.76 | loop fusion | flops 12288000 | bytes 30723072 | tf_op jit(solution)/shard_map/convert_element_type | solution.py:207
  429.5 6.8 convolution_convert_fusion.3
  436.4 75.3 %reduce-scatter.9.cloned.1.call-done = f32[1000,768]{1,0:T(8,128)} async-done(((f32[4000,768]{1,0:T(8,128)}), f32[1000,768]{1,0:T(8,128)}) %reduce-scatter.9.cloned.1.call-update) | async-done | bytes 3072016 | tf_op jit(solution)/shard_map/reduce_scatter | solution.py:225
  514.6 56.9 %reduce-scatter.7.cloned.1.call-done = bf16[1000,768]{1,0:T(8,128)(2,1)} async-done(((bf16[4000,768]{1,0:T(8,128)(2,1)}), bf16[1000,768]{1,0:T(8,128)(2,1)}) %reduce-scatter.7.cloned.1.call-update) | async-done | bytes 1536016 | tf_op jit(solution)/shard_map/reduce_scatter | solution.py:209
  580.2 43.9 %all-gather.11.cloned.1.call-done = bf16[4000,768]{1,0:T(8,128)(2,1)} async-done(((bf16[1000,768]{1,0:T(8,128)(2,1)}), bf16[4000,768]{1,0:T(8,128)(2,1)}) %all-gather.11.cloned.1.call-update) | async-done | bytes 6144016 | tf_op jit(solution)/shard_map/all_gather | solution.py:232
  624.1 6.0 convolution_convert_fusion.4
  630.1 6.7 reshape.242
  644.0 85.4 %while.32 = (s32[]{:T(128)}, f32[3,200,200]{1,2,0:T(8,128)}, bf16[4,5,200,3,64]{2,4,3,1,0:T(8,128)(2,1)}, bf16[4,5,200,3,64]{2,4,3,1,0:T(8,128)(2,1)}, bf16[4,5,...) while((s32[]{:T(128)}, f32[3,200,200]{1,2,0:T(8,128)}, ...), condition=%wide.wide.region_16.17_spmd.clone, body=%wide.wide.region_13.16_spmd.clone.sunk | while | flops 392062016 | bytes 36752904 | solution.py:120
  757.6 9.4 convolution_convert_fusion.2
  767.7 10.0 fusion.100
  777.7 10.6 fusion.101
  789.2 5.1 fusion.99
  794.4 7.8 fusion.102
  806.3 23.4 %fusion.57 = f32[732,6]{0,1:T(8,128)S(1)} fusion(s32[40000]{0:T(1024)} %copy-done.36, bf16[3,40000]{1,0:T(4,128)(2,1)S(1)} %get-tuple-element.344, bf16[3,40000]{1,0:T(4,128)(2,1)} %get-tuple-element.345), kind=kOutput, calls=%fused_computation.67 | convolution fusion | flops 381600000 | bytes 657568 | tf_op jit(solution)/shard_map/dot_general | solution.py:40
  829.8 39.7 %all-reduce.1 = (f32[192]{0:T(256)}, f32[192]{0:T(256)}, f32[732,3]{0,1:T(4,128)}, f32[768]{0:T(1024)}) all-reduce(f32[192]{0:T(256)S(1)} %reduce_sum.245, f32[192]{0:T(256)S(1)} %reduce_sum.247, f32[732,3]{0,1:T(4,128)S(1)} %slice_add_fusion.2, f32[768]{0:T(1024)S(1)} %copy-done.55), channel_id=1, replica_groups=mesh['dp'=8,'mp'=4] {'dp'}, use_global_device_ids=true, to_apply=%region_27.28 | all-reduce | flops 3348 | bytes 26784 | tf_op jit(solution)/shard_map/psum | solution.py:262
  888.4 41.2 %all-reduce = (f32[8,768]{1,0:T(8,128)}, f32[768]{0:T(1024)}, f32[768]{0:T(1024)}, f32[768]{0:T(1024)}, f32[768]{0:T(1024)}, /*index=5*/f32[768]{0:T(1024)}, f32[768]{0:T(1024)}, f32[768]{0:T(1024)}, f32[768]{0:T(1024)}) all-reduce(f32[8,768]{1,0:T(8,128)S(1)} %fusion.77, ...), channel_id=1, replica_groups=mesh['dp'=8,'mp'=4] {'dp','mp'}, use_global_device_ids=true, to_apply=%region_20.21 | all-reduce | flops 12288 | bytes 98304 | tf_op jit(solution)/shard_map/psum | solution.py:286
  929.6 138.8 %all-reduce.5.cloned.1.call-done = (f32[768,3,192]{0,2,1:T(8,128)}, f32[192,768]{1,0:T(8,128)}, f32[768,768]{1,0:T(8,128)}, f32[768,768]{1,0:T(8,128)}) async-done(((f32[768,3,192]{0,2,1:T(8,128)}, f32[192,768]{1,0:T(8,128)}, f32[768,768]{1,0:T(8,128)}, f32[768,768]{1,0:T(8,128)}), (f32[768,3,192]{0,2,1:T(8,128)}, f32[192,768]{1,0:T(8,128)}, f32[768,768]{1,0:T(8,128)}, ...) | async-done | bytes 7077904 | tf_op jit(solution)/shard_map/psum | solution.py:262
  (298 shorter events, 255.3 us)
Async XLA Ops:
  7.2 360.8 %copy-start = (bf16[768,768]{1,0:T(8,128)(2,1)S(1)}, bf16[768,768]{1,0:T(8,128)(2,1)}, u32[]{:S(2)}) copy-start(bf16[768,768]{1,0:T(8,128)(2,1)} %param.46) | copy-start | bytes 3538948
  7.2 63.3 %all-gather.5.cloned.1.call-start = ((), (), s32[]{:S(2)}) async-start(), calls=%async_computation.4 | async-start | bytes 7680000 | tf_op jit(solution)/shard_map/all_gather | solution.py:186
  9.0 254.7 %copy-start.31 = (f32[1000]{0:T(1024)}, f32[1000]{0:T(1024)S(1)}, u32[]{:S(2)}) copy-start(f32[1000]{0:T(1024)S(1)} %reshape.234) | copy-start | bytes 12004
  9.0 254.7 %copy-start.34 = (f32[1000]{0:T(1024)}, f32[1000]{0:T(1024)S(1)}, u32[]{:S(2)}) copy-start(f32[1000]{0:T(1024)S(1)} %broadcast_subtract_fusion) | copy-start | bytes 12004
  10.0 253.8 %copy-start.25 = (f32[5,768]{1,0:T(8,128)}, f32[5,768]{1,0:T(8,128)S(1)}, u32[]{:S(2)}) copy-start(f32[5,768]{1,0:T(8,128)S(1)} %fusion.86) | copy-start | bytes 46084
  18.1 23.5 %copy-start.44 = (f32[1000]{0:T(1024)}, f32[1000]{0:T(1024)S(1)}, u32[]{:S(2)}) copy-start(f32[1000]{0:T(1024)S(1)} %multiply_reduce_fusion.5) | copy-start | bytes 12004
  18.2 23.4 %copy-start.39 = (f32[1000]{0:T(1024)}, f32[1000]{0:T(1024)S(1)}, u32[]{:S(2)}) copy-start(f32[1000]{0:T(1024)S(1)} %fusion.87) | copy-start | bytes 12004
  22.1 241.7 %reduce-scatter.5.cloned.1.call-start = ((), (), s32[]{:S(2)}) async-start(), calls=%async_computation.5 | async-start | bytes 15360000 | tf_op jit(solution)/shard_map/reduce_scatter | solution.py:198
  22.6 18.9 %copy-start.36 = (s32[40000]{0:T(1024)}, s32[40000]{0:T(1024)S(1)}, u32[]{:S(2)}) copy-start(s32[40000]{0:T(1024)S(1)} %eq.35) | copy-start | bytes 480004
  22.6 21.7 %copy-start.46 = (s32[20,200]{1,0:T(8,128)S(1)}, s32[20,200]{1,0:T(8,128)}, u32[]{:S(2)}) copy-start(s32[20,200]{1,0:T(8,128)} %param.31) | copy-start | bytes 48004
  166.4 97.3 %copy-start.48 = (f32[768]{0:T(1024)S(1)}, f32[768]{0:T(1024)}, u32[]{:S(2)}) copy-start(f32[768]{0:T(1024)} %param.40) | copy-start | bytes 9220
  166.4 97.3 %copy-start.51 = (f32[768]{0:T(1024)S(1)}, f32[768]{0:T(1024)}, u32[]{:S(2)}) copy-start(f32[768]{0:T(1024)} %param.41) | copy-start | bytes 9220
  166.5 153.9 %all-gather.7.cloned.1.call-start = ((), (), s32[]{:S(2)}) async-start(), calls=%async_computation.6 | async-start | bytes 7680000 | tf_op jit(solution)/shard_map/all_gather | solution.py:203
  274.7 93.3 %all-gather.9.cloned.1.call-start = ((), (), s32[]{:S(2)}) async-start(), calls=%async_computation.8 | async-start | bytes 7680000 | tf_op jit(solution)/shard_map/all_gather | solution.py:218
  276.9 234.8 %reduce-scatter.9.cloned.1.call-start = ((), (), s32[]{:S(2)}) async-start(), calls=%async_computation.9 | async-start | bytes 15360000 | tf_op jit(solution)/shard_map/reduce_scatter | solution.py:225
  334.2 72.3 %copy-start.60 = (bf16[768,768]{1,0:T(8,128)(2,1)S(1)}, bf16[768,768]{1,0:T(8,128)(2,1)}, u32[]{:S(2)}) copy-start(bf16[768,768]{1,0:T(8,128)(2,1)} %param.44) | copy-start | bytes 3538948
  414.5 157.1 %reduce-scatter.7.cloned.1.call-start = ((), (), s32[]{:S(2)}) async-start(), calls=%async_computation.7 | async-start | bytes 7680000 | tf_op jit(solution)/shard_map/reduce_scatter | solution.py:209
  436.3 75.4 %copy-start.4 = (f32[1000,768]{1,0:T(8,128)S(1)}, f32[1000,768]{1,0:T(8,128)}, u32[]{:S(2)}) copy-start(f32[1000,768]{1,0:T(8,128)} %multiply_add_fusion) | copy-start | bytes 9216004
  436.3 135.2 %copy-start.50 = (f32[768]{0:T(1024)S(1)}, f32[768]{0:T(1024)}, u32[]{:S(2)}) copy-start(f32[768]{0:T(1024)} %param.47) | copy-start | bytes 9220
  436.3 187.7 %all-gather.11.cloned.1.call-start = ((), (), s32[]{:S(2)}) async-start(), calls=%async_computation.10 | async-start | bytes 7680000 | tf_op jit(solution)/shard_map/all_gather | solution.py:232
  575.9 48.1 %copy-start.30 = (bf16[192,768]{1,0:T(8,128)(2,1)S(1)}, bf16[192,768]{1,0:T(8,128)(2,1)}, u32[]{:S(2)}) copy-start(bf16[192,768]{1,0:T(8,128)(2,1)} %param.39) | copy-start | bytes 884740
  578.4 291.1 %reduce-scatter.11.cloned.1.call-start = ((), (), s32[]{:S(2)}) async-start(), calls=%async_computation.11 | async-start | bytes 7680000 | tf_op jit(solution)/shard_map/reduce_scatter | solution.py:242
  767.0 301.4 %all-reduce.5.cloned.1.call-start = ((), (), s32[]{:S(2)}) async-start(), calls=%async_computation.12 | async-start | bytes 14155776 | tf_op jit(solution)/shard_map/psum | solution.py:262
  777.7 11.5 %copy-start.19 = (bf16[4000,192]{0,1:T(8,128)(2,1)S(1)}, bf16[4000,192]{0,1:T(8,128)(2,1)}, u32[]{:S(2)}) copy-start(bf16[4000,192]{0,1:T(8,128)(2,1)} %reshape.241) | copy-start | bytes 4608004
  806.3 23.5 %copy-start.55 = (f32[768]{0:T(1024)S(1)}, f32[768]{0:T(1024)}, u32[]{:S(2)}) copy-start(f32[768]{0:T(1024)} %get-tuple-element.341) | copy-start | bytes 9220
  806.3 63.2 %copy-start.5 = (f32[1000,768]{1,0:T(8,128)S(1)}, f32[1000,768]{1,0:T(8,128)}, u32[]{:S(2)}) copy-start(f32[1000,768]{1,0:T(8,128)} %multiply_add_fusion.1) | copy-start | bytes 9216004
  806.3 63.2 %copy-start.26 = (f32[5,768]{1,0:T(8,128)S(1)}, f32[5,768]{1,0:T(8,128)}, u32[]{:S(2)}) copy-start(f32[5,768]{1,0:T(8,128)} %copy-done.25) | copy-start | bytes 46084
  806.3 63.2 %copy-start.32 = (f32[1000]{0:T(1024)S(1)}, f32[1000]{0:T(1024)}, u32[]{:S(2)}) copy-start(f32[1000]{0:T(1024)} %copy-done.31) | copy-start | bytes 12004
  806.3 63.2 %copy-start.35 = (f32[1000]{0:T(1024)S(1)}, f32[1000]{0:T(1024)}, u32[]{:S(2)}) copy-start(f32[1000]{0:T(1024)} %copy-done.34) | copy-start | bytes 12004
  806.3 63.2 %copy-start.38 = (f32[1000]{0:T(1024)S(1)}, f32[1000]{0:T(1024)}, u32[]{:S(2)}) copy-start(f32[1000]{0:T(1024)} %copy-done.37) | copy-start | bytes 12004
  806.3 63.2 %copy-start.40 = (f32[1000]{0:T(1024)S(1)}, f32[1000]{0:T(1024)}, u32[]{:S(2)}) copy-start(f32[1000]{0:T(1024)} %copy-done.39) | copy-start | bytes 12004
  806.3 63.2 %copy-start.43 = (f32[768]{0:T(1024)S(1)}, f32[768]{0:T(1024)}, u32[]{:S(2)}) copy-start(f32[768]{0:T(1024)} %param.33) | copy-start | bytes 9220
  (48 other events, 195.4 us)
Sparse Core Ops, SparseCore 0:
  22.2 48.2 all-gather.4
  166.6 97.1 reduce-scatter.4
  274.8 45.5 all-gather.6
  322.4 45.5 all-gather.8
  414.6 97.0 reduce-scatter.8
  514.1 57.3 reduce-scatter.6
  578.5 45.5 all-gather.10
  767.1 57.3 reduce-scatter.10
  830.7 237.6 all-reduce.4
where the time goes:
time: 1090 us; the launch traced here: 1080 us
  waiting for transfers between devices  515 us (47%)
  matrix products  252 us (23%)
  local copies, waits for them, and re-layouts  130 us (12%)
  other arithmetic  87.4 us (8%)
  blocking collectives  80.9 us (7%)
  between operations  14.8 us (1%)
    psum x1, waiting for transfers between devices, local(): lax.psum((qkv_grad, qbias_grad, vbias_grad, table_grad, out_grad, up_grad...  139 us
    reduce_scatter x1, waiting for transfers between devices, local(): attn_sum = lax.psum_scatter(out_part, 'mp', scatter_dimension=0, tiled=True)  97.1 us
    reduce_scatter x1, waiting for transfers between devices, local(): lax.psum_scatter(norm2_part, 'mp', scatter_dimension=0, tiled=True)  75.3 us
    dot_general x4, matrix products, product_last(): lax.dot_general(left, right, (((1,), (1,)), ((), ())), preferred_element_...  59.3 us
    reduce_scatter x1, waiting for transfers between devices, local(): lax.psum_scatter(down_part.astype(jnp.bfloat16), 'mp', scatter_dimension=...  56.9 us
    all_gather x1, waiting for transfers between devices, local(): grad_attn_all = lax.all_gather(grad_attn, 'mp', axis=0, tiled=True)  43.9 us
    all_gather x1, waiting for transfers between devices, local(): mlp_in = lax.all_gather(normed2, 'mp', axis=0, tiled=True)  43.4 us
    dot_general x2, matrix products, product_cross(): lax.dot_general(left, right, (((0,), (1,)), ((), ())), preferred_element_...  42.3 us
  transfers between devices with their start and end apart: 9, of which 8 were waited for; matrix products, arithmetic and copies ran while one was open for 13% of the time, Pallas kernels for 0%

commit v1 on v0

--- a/solution.py
+++ b/solution.py
@@ -7,6 +7,18 @@
 SEQ = 200
 GROUPS = 8
 IMG_BLK = 5
+
+
+def gather_by_bits(x, axis, dim):
+    ways, here, step = (lax.axis_size(axis), lax.axis_index(axis), x.shape[dim])
+    line, have = (x, 1)
+    while have < ways:
+        line = jnp.concatenate(
+            [line, lax.ppermute(line, axis, [(d, (d - have) % ways) for d in range(ways)])],
+            axis=dim,
+        )
+        have = 2 * have
+    return jnp.roll(line, here * step, axis=dim)
 
 
 def layer_norm(values, gain, shift):
@@ -200,7 +212,7 @@
     middle = start + gamma_attn * attn_value
     norm2_value, norm2_back = jax.vjp(layer_norm, middle, norm2_gain, norm2_shift)
     normed2 = norm2_value.astype(jnp.bfloat16)
-    mlp_in = lax.all_gather(normed2, "mp", axis=0, tiled=True)
+    mlp_in = gather_by_bits(normed2, "mp", 0)
     up_all, upb_all, down_all = (up_weight, up_bias, down_weight)
     hidden_pre = product(mlp_in, up_all) + upb_all.astype(jnp.float32)
     hidden_act, gelu_back = jax.vjp(gelu_exact, hidden_pre)

time: 1090 us -> 1140 us (1.046)
  waiting for transfers between devices: 515 us -> 550 us
  local copies, waits for them, and re-layouts: 130 us -> 144 us
    ppermute x0 -> x2, waiting for transfers between devices: none -> 113 us  [gather_by_bits(): lax.ppermute(line, axis, [(d, (d - have) % ways) for d in range(ways)])]
    all_gather x1 -> x0, waiting for transfers between devices: 43.4 us -> none  [local(): mlp_in = lax.all_gather(normed2, 'mp', axis=0, tiled=True)]
    all_gather x1, waiting for transfers between devices: 33.8 us -> 0.01 us  [local(): grad_mlp_all = lax.all_gather(grad_mlp, 'mp', axis=0, tiled=True)]
    unnamed x141 -> x151, local copies, waits for them, and re-layouts: 22.3 us -> 33 us
  transfers between devices with their start and end apart: 9 -> 10, of which waited for: 8 -> 8; matrix products, arithmetic and copies ran while one was open for 13% -> 14% of each run, Pallas kernels for 0% -> 0%
where the time goes in v1:
time: 1140 us; the launch traced here: 1130 us
  waiting for transfers between devices  550 us (48%)
  matrix products  249 us (22%)
  local copies, waits for them, and re-layouts  144 us (13%)
  other arithmetic  89.7 us (8%)
  blocking collectives  81.1 us (7%)
  between operations  15.1 us (1%)
    psum x1, waiting for transfers between devices, local(): lax.psum((qkv_grad, qbias_grad, vbias_grad, table_grad, out_grad, up_grad...  139 us
    ppermute x2, waiting for transfers between devices, gather_by_bits(): lax.ppermute(line, axis, [(d, (d - have) % ways) for d in range(ways)])  113 us
    reduce_scatter x1, waiting for transfers between devices, local(): attn_sum = lax.psum_scatter(out_part, 'mp', scatter_dimension=0, tiled=True)  92.7 us
    reduce_scatter x1, waiting for transfers between devices, local(): lax.psum_scatter(norm2_part, 'mp', scatter_dimension=0, tiled=True)  78.8 us
    dot_general x4, matrix products, product_last(): lax.dot_general(left, right, (((1,), (1,)), ((), ())), preferred_element_...  59.3 us
    reduce_scatter x1, waiting for transfers between devices, local(): lax.psum_scatter(down_part.astype(jnp.bfloat16), 'mp', scatter_dimension=...  56.9 us
    all_gather x1, waiting for transfers between devices, local(): grad_attn_all = lax.all_gather(grad_attn, 'mp', axis=0, tiled=True)  43.9 us
    dot_general x2, matrix products, product_cross(): lax.dot_general(left, right, (((0,), (1,)), ((), ())), preferred_element_...  42.3 us
  transfers between devices with their start and end apart: 10, of which 8 were waited for; matrix products, arithmetic and copies ran while one was open for 14% of the time, Pallas kernels for 0%

profile of v1, /device:TPU:0, one launch (start us, length us, event | category | flops | bytes accessed | tf_op | source)
XLA Modules:
  0.0 1132.3 jit_solution(5210485426724552212)
XLA Ops:
  22.6 18.9 %fusion.61 = f32[3,40000]{1,0:T(4,128)} fusion(bf16[732,3]{0,1:T(4,128)(2,1)S(1)} %copy-done.65, s32[40000]{0:T(1024)S(1)} %eq.38), kind=kOutput, calls=%fused_computation.71 | convolution fusion | flops 204960000 | bytes 644392 | tf_op jit(solution)/shard_map/dot_general | solution.py:52
  44.3 26.1 %all-gather.4.cloned.1.call-done = bf16[4000,768]{1,0:T(8,128)(2,1)} async-done(((bf16[1000,768]{1,0:T(8,128)(2,1)}), bf16[4000,768]{1,0:T(8,128)(2,1)}) %all-gather.4.cloned.1.call-update) | async-done | bytes 6144016 | tf_op jit(solution)/shard_map/all_gather | solution.py:198
  70.5 6.2 fusion.101
  80.6 7.2 reshape.237
  92.3 7.4 reshape.239
  104.2 7.2 reshape.240
  117.5 30.9 %while.31 = (s32[]{:T(128)}, bf16[4,5,200,3,64]{2,4,3,1,0:T(8,128)(2,1)}, f32[4,5,3,200,1]{3,2,1,4,0:T(4,128)}, bf16[4,5,200,3,64]{2,4,3,1,0:T(8,128)(2,1)}, s32...) while((s32[]{:T(128)}, ...), condition=%wide.wide.region_5.6_spmd, body=%wide.wide.region_2.5_spmd.sunk | while | flops 160390000 | bytes 11681225 | solution.py:94
  152.9 5.7 reshape.241
  158.6 7.7 fusion.102
  171.0 92.7 %reduce-scatter.5.cloned.1.call-done = f32[1000,768]{1,0:T(8,128)} async-done(((f32[4000,768]{1,0:T(8,128)}), f32[1000,768]{1,0:T(8,128)}) %reduce-scatter.5.cloned.1.call-update) | async-done | bytes 3072016 | tf_op jit(solution)/shard_map/reduce_scatter | solution.py:210
  275.1 48.9 %collective-permute-done = bf16[1000,768]{1,0:T(8,128)(2,1)S(1)} collective-permute-done((bf16[1000,768]{1,0:T(8,128)(2,1)S(1)}, bf16[1000,768]{1,0:T(8,128)(2,1)S(1)}, u32[]{:S(2)}, u32[]{:S(2)}) %collective-permute-start) | collective-permute-done | bytes 1536032 | tf_op jit(solution)/shard_map/ppermute | solution.py:17
  330.4 64.3 %collective-permute-done.1 = bf16[2000,768]{1,0:T(8,128)(2,1)} collective-permute-done((bf16[2000,768]{1,0:T(8,128)(2,1)}, bf16[2000,768]{1,0:T(8,128)(2,1)}, u32[]{:S(2)}, u32[]{:S(2)}) %collective-permute-start.1) | collective-permute-done | bytes 3072032 | tf_op jit(solution)/shard_map/ppermute | solution.py:17
  405.4 10.5 fusion.70
  415.9 35.9 %convert_reduce_fusion.1 = (f32[768]{0:T(1024)}, bf16[4000,768]{1,0:T(8,128)(2,1)S(1)}, f32[4000,768]{1,0:T(8,128)}) fusion(f32[4000,768]{1,0:T(8,128)} %fusion.70, f32[768]{0:T(1024)S(1)} %convert_element_type.138, bf16[4000,768]{1,0:T(8,128)(2,1)} %all-gather.6.cloned.1.call-done, bf16[768,768]{1,0:T(8,128)(2,1)S(1)} %copy-done), kind=kOutput, calls=%fused_computation.74 | convolution fusion | flops 4948990976 | bytes 38049792 | tf_op jit(solution)/shard_map/dot_general | solution.py:46
  454.4 7.9 fusion.103
  462.6 9.7 multiply_convert_fusion.1
  476.1 6.8 convolution_convert_fusion.3
  483.0 78.8 %reduce-scatter.9.cloned.1.call-done = f32[1000,768]{1,0:T(8,128)} async-done(((f32[4000,768]{1,0:T(8,128)}), f32[1000,768]{1,0:T(8,128)}) %reduce-scatter.9.cloned.1.call-update) | async-done | bytes 3072016 | tf_op jit(solution)/shard_map/reduce_scatter | solution.py:237
  564.7 56.9 %reduce-scatter.7.cloned.1.call-done = bf16[1000,768]{1,0:T(8,128)(2,1)} async-done(((bf16[4000,768]{1,0:T(8,128)(2,1)}), bf16[1000,768]{1,0:T(8,128)(2,1)}) %reduce-scatter.7.cloned.1.call-update) | async-done | bytes 1536016 | tf_op jit(solution)/shard_map/reduce_scatter | solution.py:221
  630.2 43.9 %all-gather.8.cloned.1.call-done = bf16[4000,768]{1,0:T(8,128)(2,1)} async-done(((bf16[1000,768]{1,0:T(8,128)(2,1)}), bf16[4000,768]{1,0:T(8,128)(2,1)}) %all-gather.8.cloned.1.call-update) | async-done | bytes 6144016 | tf_op jit(solution)/shard_map/all_gather | solution.py:244
  674.1 6.0 convolution_convert_fusion.4
  680.1 6.6 reshape.242
  693.8 85.5 %while.32 = (s32[]{:T(128)}, f32[3,200,200]{1,2,0:T(8,128)}, bf16[4,5,200,3,64]{2,4,3,1,0:T(8,128)(2,1)}, bf16[4,5,200,3,64]{2,4,3,1,0:T(8,128)(2,1)}, bf16[4,5,...) while((s32[]{:T(128)}, f32[3,200,200]{1,2,0:T(8,128)}, ...), condition=%wide.wide.region_16.17_spmd.clone, body=%wide.wide.region_13.16_spmd.clone.sunk | while | flops 392062016 | bytes 36752904 | solution.py:132
  792.1 5.4 reshape.244
  807.8 9.4 convolution_convert_fusion.2
  818.0 10.0 fusion.68
  828.0 10.6 fusion.105
  844.7 7.8 fusion.106
  856.6 23.4 %fusion.57 = f32[732,6]{0,1:T(8,128)S(1)} fusion(s32[40000]{0:T(1024)} %copy-done.37, bf16[3,40000]{1,0:T(4,128)(2,1)S(1)} %get-tuple-element.344, bf16[3,40000]{1,0:T(4,128)(2,1)} %get-tuple-element.345), kind=kOutput, calls=%fused_computation.67 | convolution fusion | flops 381600000 | bytes 657568 | tf_op jit(solution)/shard_map/dot_general | solution.py:52
  880.0 39.9 %all-reduce.1 = (f32[192]{0:T(256)}, f32[192]{0:T(256)}, f32[732,3]{0,1:T(4,128)}, f32[768]{0:T(1024)}) all-reduce(f32[192]{0:T(256)S(1)} %reduce_sum.245, f32[192]{0:T(256)S(1)} %reduce_sum.247, f32[732,3]{0,1:T(4,128)S(1)} %slice_add_fusion.2, f32[768]{0:T(1024)S(1)} %copy-done.59), channel_id=1, replica_groups=mesh['dp'=8,'mp'=4] {'dp'}, use_global_device_ids=true, to_apply=%region_27.28 | all-reduce | flops 3348 | bytes 26784 | tf_op jit(solution)/shard_map/psum | solution.py:274
  938.7 41.2 %all-reduce = (f32[8,768]{1,0:T(8,128)}, f32[768]{0:T(1024)}, f32[768]{0:T(1024)}, f32[768]{0:T(1024)}, f32[768]{0:T(1024)}, /*index=5*/f32[768]{0:T(1024)}, f32[768]{0:T(1024)}, f32[768]{0:T(1024)}, f32[768]{0:T(1024)}) all-reduce(f32[8,768]{1,0:T(8,128)S(1)} %fusion.81, ...), channel_id=1, replica_groups=mesh['dp'=8,'mp'=4] {'dp','mp'}, use_global_device_ids=true, to_apply=%region_20.21 | all-reduce | flops 12288 | bytes 98304 | tf_op jit(solution)/shard_map/psum | solution.py:298
  979.9 138.8 %all-reduce.5.cloned.1.call-done = (f32[768,3,192]{0,2,1:T(8,128)}, f32[192,768]{1,0:T(8,128)}, f32[768,768]{1,0:T(8,128)}, f32[768,768]{1,0:T(8,128)}) async-done(((f32[768,3,192]{0,2,1:T(8,128)}, f32[192,768]{1,0:T(8,128)}, f32[768,768]{1,0:T(8,128)}, f32[768,768]{1,0:T(8,128)}), (f32[768,3,192]{0,2,1:T(8,128)}, f32[192,768]{1,0:T(8,128)}, f32[768,768]{1,0:T(8,128)}, ...) | async-done | bytes 7077904 | tf_op jit(solution)/shard_map/psum | solution.py:274
  (311 shorter events, 275.5 us)
Async XLA Ops:
  7.2 408.7 %copy-start = (bf16[768,768]{1,0:T(8,128)(2,1)S(1)}, bf16[768,768]{1,0:T(8,128)(2,1)}, u32[]{:S(2)}) copy-start(bf16[768,768]{1,0:T(8,128)(2,1)} %param.46) | copy-start | bytes 3538948
  7.2 63.3 %all-gather.4.cloned.1.call-start = ((), (), s32[]{:S(2)}) async-start(), calls=%async_computation.4 | async-start | bytes 7680000 | tf_op jit(solution)/shard_map/all_gather | solution.py:198
  9.0 254.6 %copy-start.32 = (f32[1000]{0:T(1024)}, f32[1000]{0:T(1024)S(1)}, u32[]{:S(2)}) copy-start(f32[1000]{0:T(1024)S(1)} %reshape.234) | copy-start | bytes 12004
  9.0 254.6 %copy-start.35 = (f32[1000]{0:T(1024)}, f32[1000]{0:T(1024)S(1)}, u32[]{:S(2)}) copy-start(f32[1000]{0:T(1024)S(1)} %broadcast_subtract_fusion) | copy-start | bytes 12004
  10.0 253.7 %copy-start.26 = (f32[5,768]{1,0:T(8,128)}, f32[5,768]{1,0:T(8,128)S(1)}, u32[]{:S(2)}) copy-start(f32[5,768]{1,0:T(8,128)S(1)} %fusion.90) | copy-start | bytes 46084
  18.1 23.5 %copy-start.45 = (f32[1000]{0:T(1024)}, f32[1000]{0:T(1024)S(1)}, u32[]{:S(2)}) copy-start(f32[1000]{0:T(1024)S(1)} %multiply_reduce_fusion.5) | copy-start | bytes 12004
  18.2 23.4 %copy-start.40 = (f32[1000]{0:T(1024)}, f32[1000]{0:T(1024)S(1)}, u32[]{:S(2)}) copy-start(f32[1000]{0:T(1024)S(1)} %fusion.91) | copy-start | bytes 12004
  22.1 241.5 %reduce-scatter.5.cloned.1.call-start = ((), (), s32[]{:S(2)}) async-start(), calls=%async_computation.5 | async-start | bytes 15360000 | tf_op jit(solution)/shard_map/reduce_scatter | solution.py:210
  166.3 97.3 %copy-start.50 = (f32[768]{0:T(1024)S(1)}, f32[768]{0:T(1024)}, u32[]{:S(2)}) copy-start(f32[768]{0:T(1024)} %param.40) | copy-start | bytes 9220
  166.3 97.3 %copy-start.53 = (f32[768]{0:T(1024)S(1)}, f32[768]{0:T(1024)}, u32[]{:S(2)}) copy-start(f32[768]{0:T(1024)} %param.41) | copy-start | bytes 9220
  166.4 249.6 %all-gather.6.cloned.1.call-start = ((), (), s32[]{:S(2)}) async-start(), calls=%async_computation.7 | async-start | bytes 7680000 | tf_op jit(solution)/shard_map/all_gather | solution.py:230
  170.5 391.3 %reduce-scatter.9.cloned.1.call-start = ((), (), s32[]{:S(2)}) async-start(), calls=%async_computation.8 | async-start | bytes 15360000 | tf_op jit(solution)/shard_map/reduce_scatter | solution.py:237
  275.1 52.7 %copy-start.60 = (bf16[768]{0:T(1024)(128)(2,1)S(1)}, bf16[768]{0:T(1024)(128)(2,1)}, u32[]{:S(2)}) copy-start(bf16[768]{0:T(1024)(128)(2,1)} %param.45) | copy-start | bytes 4612
  275.1 48.9 %collective-permute-start = (bf16[1000,768]{1,0:T(8,128)(2,1)S(1)}, bf16[1000,768]{1,0:T(8,128)(2,1)S(1)}, u32[]{:S(2)}, u32[]{:S(2)}) collective-permute-start(bf16[1000,768]{1,0:T(8,128)(2,1)S(1)} %get-tuple-element.353), channel_id=1, source_target_pairs={{0,3},{1,0},{2,1},{3,2},{4,7},{5,4},{6,5},{7,6},{8,11},{9,8},{10,9... | collective-permute-start | bytes 4608008 | tf_op jit(solution)/shard_map/ppermute | solution.py:17
  326.1 68.6 %collective-permute-start.1 = (bf16[2000,768]{1,0:T(8,128)(2,1)}, bf16[2000,768]{1,0:T(8,128)(2,1)}, u32[]{:S(2)}, u32[]{:S(2)}) collective-permute-start(bf16[2000,768]{1,0:T(8,128)(2,1)} %pad_maximum_fusion), channel_id=1, source_target_pairs={{0,2},{1,3},{2,0},{3,1},{4,6},{5,7},{6,4},{7,5},{8,10},{9,11},{10,... | collective-permute-start | bytes 9216008 | tf_op jit(solution)/shard_map/ppermute | solution.py:17
  462.3 159.3 %reduce-scatter.7.cloned.1.call-start = ((), (), s32[]{:S(2)}) async-start(), calls=%async_computation.6 | async-start | bytes 7680000 | tf_op jit(solution)/shard_map/reduce_scatter | solution.py:221
  482.9 78.9 %copy-start.4 = (f32[1000,768]{1,0:T(8,128)S(1)}, f32[1000,768]{1,0:T(8,128)}, u32[]{:S(2)}) copy-start(f32[1000,768]{1,0:T(8,128)} %multiply_add_fusion) | copy-start | bytes 9216004
  482.9 138.7 %copy-start.49 = (f32[768]{0:T(1024)S(1)}, f32[768]{0:T(1024)}, u32[]{:S(2)}) copy-start(f32[768]{0:T(1024)} %param.48) | copy-start | bytes 9220
  483.0 138.7 %copy-start.52 = (f32[768]{0:T(1024)S(1)}, f32[768]{0:T(1024)}, u32[]{:S(2)}) copy-start(f32[768]{0:T(1024)} %param.47) | copy-start | bytes 9220
  483.0 191.1 %all-gather.8.cloned.1.call-start = ((), (), s32[]{:S(2)}) async-start(), calls=%async_computation.9 | async-start | bytes 7680000 | tf_op jit(solution)/shard_map/all_gather | solution.py:244
  564.7 61.3 %copy-start.54 = (f32[768]{0:T(1024)S(1)}, f32[768]{0:T(1024)}, u32[]{:S(2)}) copy-start(f32[768]{0:T(1024)} %param.41) | copy-start | bytes 9220
  626.0 48.1 %copy-start.31 = (bf16[192,768]{1,0:T(8,128)(2,1)S(1)}, bf16[192,768]{1,0:T(8,128)(2,1)}, u32[]{:S(2)}) copy-start(bf16[192,768]{1,0:T(8,128)(2,1)} %param.39) | copy-start | bytes 884740
  628.4 291.4 %reduce-scatter.11.cloned.1.call-start = ((), (), s32[]{:S(2)}) async-start(), calls=%async_computation.10 | async-start | bytes 7680000 | tf_op jit(solution)/shard_map/reduce_scatter | solution.py:254
  817.3 301.4 %all-reduce.5.cloned.1.call-start = ((), (), s32[]{:S(2)}) async-start(), calls=%async_computation.11 | async-start | bytes 14155776 | tf_op jit(solution)/shard_map/psum | solution.py:274
  856.5 23.5 %copy-start.59 = (f32[768]{0:T(1024)S(1)}, f32[768]{0:T(1024)}, u32[]{:S(2)}) copy-start(f32[768]{0:T(1024)} %get-tuple-element.341) | copy-start | bytes 9220
  856.5 63.3 %copy-start.5 = (f32[1000,768]{1,0:T(8,128)S(1)}, f32[1000,768]{1,0:T(8,128)}, u32[]{:S(2)}) copy-start(f32[1000,768]{1,0:T(8,128)} %multiply_add_fusion.1) | copy-start | bytes 9216004
  856.5 63.3 %copy-start.27 = (f32[5,768]{1,0:T(8,128)S(1)}, f32[5,768]{1,0:T(8,128)}, u32[]{:S(2)}) copy-start(f32[5,768]{1,0:T(8,128)} %copy-done.26) | copy-start | bytes 46084
  856.5 63.3 %copy-start.33 = (f32[1000]{0:T(1024)S(1)}, f32[1000]{0:T(1024)}, u32[]{:S(2)}) copy-start(f32[1000]{0:T(1024)} %copy-done.32) | copy-start | bytes 12004
  856.5 63.3 %copy-start.36 = (f32[1000]{0:T(1024)S(1)}, f32[1000]{0:T(1024)}, u32[]{:S(2)}) copy-start(f32[1000]{0:T(1024)} %copy-done.35) | copy-start | bytes 12004
  856.6 63.3 %copy-start.39 = (f32[1000]{0:T(1024)S(1)}, f32[1000]{0:T(1024)}, u32[]{:S(2)}) copy-start(f32[1000]{0:T(1024)} %copy-done.38) | copy-start | bytes 12004
  856.6 63.3 %copy-start.41 = (f32[1000]{0:T(1024)S(1)}, f32[1000]{0:T(1024)}, u32[]{:S(2)}) copy-start(f32[1000]{0:T(1024)} %copy-done.40) | copy-start | bytes 12004
  856.6 63.3 %copy-start.44 = (f32[768]{0:T(1024)S(1)}, f32[768]{0:T(1024)}, u32[]{:S(2)}) copy-start(f32[768]{0:T(1024)} %param.33) | copy-start | bytes 9220
  (52 other events, 251.5 us)
Sparse Core Ops, SparseCore 0:
  22.2 48.2 all-gather.3
  166.5 97.1 reduce-scatter.4
  265.8 61.6 all-gather.5
  462.5 99.2 reduce-scatter.8
  564.2 57.3 reduce-scatter.6
  628.5 45.5 all-gather.7
  817.4 57.3 reduce-scatter.10
  881.0 237.6 all-reduce.4
